TPU v7x, 512 devices: a whole 4x8x8 slice. The times are simulated.
512 devices in a mesh: mem: 8 (over z_hi, core), grid: 64 (over y, x, z_lo).
Axes of the slice: x: 4, y: 8, z: 8 (z_hi: 4, z_lo: 2; z = z_hi * 2 + z_lo), core: 2. Of those that a mesh axis runs over, the one named last changes fastest.
Arguments:
- control: bfloat16 [32, 32, 384, 768], P('mem', None, 'grid'), may hold values from -6 to 6
- perturbation: bfloat16 [32, 32, 768, 384], P('mem', None, 'grid'), may hold values from -6 to 6
- vertical: bfloat16 [32, 32], replicated, may hold values from 0 to 1
- lat_counts: int32 [64], replicated, may hold values from 1 to 6, 361 in all
- lon_counts: int32 [64], replicated, may hold values from 1 to 12, 720 in all
Outputs:
- increment: float32 [32, 768, 384], P('mem', 'grid')
Inputs may be any that keep to these rules, and one draw needn't show every extreme that they name: Slab g holds its first lat_counts[g] latitude slots as real rows, numbered on from the slabs before it. Slab g holds its first lon_counts[g] longitude slots as real columns, numbered on from the slabs before it.
All inputs are finite; a program needn't handle non-finite values.
Results may differ from a plain program's by a relative error of at most 0.0067.
Values may be sent and summed in bfloat16 or wider, within the bound.
A program may use at most 64 MiB of HBM per device.

v0:
```python
import jax
import jax.numpy as jnp
from jax import lax
from jax.sharding import PartitionSpec as P

LAT = 361
LON = 720
LENGTH = 8
BAND = 48


def slot_table(counts, slot_count):
    devices = counts.shape[0]
    slot_ids = jnp.arange(devices * slot_count, dtype=jnp.int32)
    device_of = slot_ids // slot_count
    offset_in = slot_ids - device_of * slot_count
    offsets = jnp.cumsum(counts) - counts
    one_hot = device_of[:, None] == jnp.arange(devices, dtype=jnp.int32)[None, :]
    count_of = jnp.sum(jnp.where(one_hot, counts[None, :], 0), axis=1)
    start_of = jnp.sum(jnp.where(one_hot, offsets[None, :], 0), axis=1)
    return (start_of + offset_in, offset_in < count_of)


def pass_matrix(counts, slot_count, extent, periodic):
    position, usable = slot_table(counts, slot_count)
    lag = position[None, :] - position[:, None]
    if periodic:
        lag = jnp.where(lag < 0, lag + extent, lag)
    steps_f = jnp.arange(0, BAND + 1).astype(jnp.float32)
    normal_sum = jnp.sqrt(jnp.sum(jnp.exp(-2.0 * steps_f / LENGTH)))
    lag_f = lag.astype(jnp.float32)
    inside = (lag >= 0) & (lag <= BAND) & usable[:, None] & usable[None, :]
    weight = jnp.where(inside, jnp.exp(-lag_f / LENGTH) / normal_sum, 0.0)
    return weight.astype(jnp.bfloat16)


def per_device(control, perturbation, vertical, lat_counts, lon_counts):
    groups = lax.axis_size("grid")
    row_slots = control.shape[2]
    lon_pad = control.shape[3]
    col_slots = lon_pad // groups
    lon_matrix = pass_matrix(lon_counts, col_slots, LON, True)
    lat_matrix = pass_matrix(lat_counts, row_slots, LAT, False)
    smooth = jnp.dot(control.reshape(-1, lon_pad), lon_matrix, preferred_element_type=jnp.float32)
    smooth = smooth.astype(jnp.bfloat16).reshape(control.shape)
    columns = lax.all_to_all(smooth, "grid", split_axis=3, concat_axis=2, tiled=True)
    filtered = jnp.einsum(
        "mljc,ji->mlci", columns, lat_matrix, preferred_element_type=jnp.float32
    ).astype(jnp.bfloat16)
    mixed = jnp.einsum("kl,mlci->mkci", vertical, filtered, preferred_element_type=jnp.float32)
    partial_value = jnp.sum(mixed * perturbation.astype(jnp.float32), axis=0)
    summed = lax.psum(partial_value, "mem")
    level_share = partial_value.shape[0] // lax.axis_size("mem")
    return lax.dynamic_slice_in_dim(summed, lax.axis_index("mem") * level_share, level_share, 0)


def solution(mesh):
    in_specs = (P("mem", None, "grid", None), P("mem", None, "grid", None), P(), P(), P())
    out_specs = P("mem", "grid", None)
    return jax.shard_map(
        per_device, mesh=mesh, in_specs=in_specs, out_specs=out_specs, check_vma=False
    )
```

profile of v0, /device:TPU:1, one launch (start us, length us, event | category | flops | bytes accessed | tf_op | source)
XLA Modules:
  0.0 178.4 jit_solution(16469525209210127878)
XLA Ops:
  6.5 0.6 exponential_reduce_fusion
  7.2 0.7 copy.27
  7.9 0.1 reduce-window.18
  8.0 0.1 reduce
  8.1 0.7 sub.95
  8.8 0.8 select_reduce_fusion
  10.3 1.9 %copy.28 = bf16[4,32,6,768]{3,2,1,0:T(8,128)(2,1)S(1)} copy(bf16[4,32,6,768]{3,1,2,0:T(8,128)(2,1)} %param.5) | data formatting | bytes 2359296 | tf_op args[0]
  12.2 0.4 reshape.168
  12.7 2.8 %fusion.11 = bf16[768,768]{1,0:T(8,128)(2,1)} fusion(bf16[768,768]{1,0:T(8,128)(2,1)S(1)} %reshape.168, f32[]{:T(128)S(6)} %sqrt.4, s32[768]{0:T(1024)S(1)} %fusion.59, pred[768]{0:T(1024)(128)(4,1)S(1)} %fusion.58), kind=kOutput, calls=%fused_computation.13 | convolution fusion | flops 915406848 | bytes 2363140 | tf_op jit(solution)/shard_map/dot_general | solution.py:44
  15.5 2.2 %reshape.169 = bf16[4,32,6,768]{3,2,1,0:T(8,128)(2,1)S(1)} reshape(bf16[768,768]{1,0:T(8,128)(2,1)} %fusion.11) | data formatting | bytes 2359296 | tf_op jit(solution)/shard_map/reshape | solution.py:45
  17.7 4.6 %copy.29 = bf16[4,32,6,768]{1,0,2,3:T(4,128)(2,1)} copy(bf16[4,32,6,768]{3,2,1,0:T(8,128)(2,1)S(1)} %reshape.169) | data formatting | bytes 2359296 | tf_op jit(solution)/shard_map/reshape | solution.py:45
  22.3 8.1 %reshape.176 = bf16[64,2,4608]{2,1,0:T(2,128)(2,1)} reshape(bf16[768,6,4,32]{3,2,1,0:T(4,128)(2,1)} %bitcast.26) | data formatting | bytes 2359296
  30.4 13.1 %all-to-all-start = ((bf16[64,2,4608]{2,1,0:T(2,128)(2,1)}), bf16[64,2,4608]{2,1,0:T(2,128)(2,1)S(1)}, u32[]{:S(2)}, u32[]{:S(2)}) async-start(bf16[64,2,4608]{2,1,0:T(2,128)(2,1)} %reshape.176), calls=%async_computation | async-start | bytes 2359296 | tf_op jit(solution)/shard_map/all_to_all | solution.py:46
  43.5 0.0 all-reduce.2.cloned.1.call-start
  43.6 0.1 copy.32
  43.7 0.1 reduce-window.19
  43.8 0.1 reduce.1
  43.9 0.1 select_reduce_fusion.2
  44.0 28.2 %all-to-all-done = bf16[64,2,4608]{2,1,0:T(2,128)(2,1)S(1)} async-done(((bf16[64,2,4608]{2,1,0:T(2,128)(2,1)}), bf16[64,2,4608]{2,1,0:T(2,128)(2,1)S(1)}, u32[]{:S(2)}, u32[]{:S(2)}) %all-to-all-start) | async-done | bytes 1179680 | tf_op jit(solution)/shard_map/all_to_all | solution.py:46
  72.2 4.1 %reshape.177 = bf16[768,6,4,32]{3,2,1,0:T(4,128)(2,1)} reshape(bf16[64,2,4608]{2,1,0:T(2,128)(2,1)S(1)} %all-to-all-done) | data formatting | bytes 2359296
  76.3 6.2 %copy.31 = bf16[4,32,64,6,12]{1,0,4,3,2:T(4,128)(2,1)} copy(bf16[4,32,64,6,12]{1,0,3,4,2:T(4,128)(2,1)} %bitcast.27) | data formatting | bytes 2359296 | tf_op jit(solution)/shard_map/all_to_all | solution.py:46
  82.5 5.9 %fusion.2 = f32[32,12,384]{2,0,1:T(8,128)} fusion(bf16[4,32,12,384]{3,1,2,0:T(8,128)(2,1)S(1)} %copy-done.2, bf16[4,32,384,12]{1,0,3,2:T(4,128)(2,1)} %bitcast.28, f32[]{:T(128)S(6)} %sqrt.4, s32[384]{0:T(512)S(1)} %fusion.64, pred[384]{0:T(512)(128)(4,1)S(1)} %fusion.63, bf16[32,32]{1,0:T(8,128)(2,1)S(1)} %copy-done), kind=kOutput, calls=%fused_computation.4 | convolution fusion | flops 494714880 | bytes 2953092 | tf_op jit(solution)/shard_map/kl,mlci->mkci/dot_general | solution.py:50
  88.4 81.6 %all-reduce.2.cloned.1.call-done = f32[32,12,384]{2,0,1:T(8,128)} async-done(((f32[32,12,384]{2,0,1:T(8,128)}), f32[32,12,384]{2,0,1:T(8,128)}) %all-reduce.2.cloned.1.call-update) | async-done | bytes 589840 | tf_op jit(solution)/shard_map/psum | solution.py:52
  170.0 1.6 constant_dynamic-slice_fusion
  (14 shorter events, 0.1 us)
Async XLA Ops:
  6.5 75.9 %copy-start = (bf16[32,32]{1,0:T(8,128)(2,1)S(1)}, bf16[32,32]{1,0:T(8,128)(2,1)}, u32[]{:S(2)}) copy-start(bf16[32,32]{1,0:T(8,128)(2,1)} %param.7) | copy-start | bytes 6148
  30.4 13.1 %copy-start.1 = (s32[64]{0:T(128)S(1)}, s32[64]{0:T(128)}, u32[]{:S(2)}) copy-start(s32[64]{0:T(128)} %param.8) | copy-start | bytes 772
  30.4 41.8 %all-to-all-start = ((bf16[64,2,4608]{2,1,0:T(2,128)(2,1)}), bf16[64,2,4608]{2,1,0:T(2,128)(2,1)S(1)}, u32[]{:S(2)}, u32[]{:S(2)}) async-start(bf16[64,2,4608]{2,1,0:T(2,128)(2,1)} %reshape.176), calls=%async_computation | async-start | bytes 2359296 | tf_op jit(solution)/shard_map/all_to_all | solution.py:46
  43.5 126.5 %all-reduce.2.cloned.1.call-start = ((), (), s32[]{:S(2)}) async-start(), calls=%async_computation.1 | async-start | bytes 1179648 | tf_op jit(solution)/shard_map/psum | solution.py:52
  76.3 6.2 %copy-start.2 = (bf16[4,32,12,384]{3,1,2,0:T(8,128)(2,1)S(1)}, bf16[4,32,12,384]{3,1,2,0:T(8,128)(2,1)}, u32[]{:S(2)}) copy-start(bf16[4,32,12,384]{3,1,2,0:T(8,128)(2,1)} %param.6) | copy-start | bytes 3538948
Sparse Core Ops, SparseCore 0:
  88.5 81.4 all-reduce.1
where the time goes:
time: 179 us; the launch traced here: 178 us
  waiting for transfers between devices  110 us (61%)
  local copies, waits for them, and re-layouts  30 us (17%)
  between operations  14.2 us (8%)
  starting transfers between devices  13.1 us (7%)
  matrix products  8.74 us (5%)
  other arithmetic  2.63 us (1%)
    psum x1, waiting for transfers between devices, per_device(): summed = lax.psum(partial_value, 'mem')  81.6 us
    all_to_all x1, waiting for transfers between devices, per_device(): lax.all_to_all(smooth, 'grid', split_axis=3, concat_axis=2, tiled=True)  28.2 us
    unnamed x9, local copies, waits for them, and re-layouts  14.2 us
    all_to_all x1, starting transfers between devices, per_device(): lax.all_to_all(smooth, 'grid', split_axis=3, concat_axis=2, tiled=True)  13.1 us
    reshape x2, local copies, waits for them, and re-layouts, per_device(): smooth = smooth.astype(jnp.bfloat16).reshape(control.shape)  6.78 us
    all_to_all x1, local copies, waits for them, and re-layouts, per_device(): lax.all_to_all(smooth, 'grid', split_axis=3, concat_axis=2, tiled=True)  6.17 us
    dot_general x1, matrix products, per_device(): jnp.einsum('kl,mlci->mkci', vertical, filtered, preferred_element_type=jn...  5.89 us
  transfers between devices with their start and end apart: 2, of which 2 were waited for; matrix products, arithmetic and copies ran while one was open for 0% of the time, Pallas kernels for 0%

commit v1 on v0

v1 whole, which is shorter than its diff:
```python
import math

import jax
import jax.numpy as jnp
import numpy as np
from jax import lax
from jax.experimental import pallas as pl
from jax.experimental.pallas import tpu as pltpu
from jax.sharding import PartitionSpec as P

LAT = 361
LON = 720
LENGTH = 8
BAND = 48
MESH = pl.DeviceIdType.MESH
FAR = 20000.0
NORM = np.sqrt(np.sum(np.exp(np.float32(-2.0) * np.arange(BAND + 1, dtype=np.float32) / np.float32(LENGTH)), dtype=np.float32))
SCALE = float(np.float32(1.0) / NORM)

GRID = 64
MEM = 8
MEMBERS = 4
LEV = 32
ROWS = 6
COLS = 12
LON_PAD = GRID * COLS
LAT_PAD = GRID * ROWS
LANES = MEMBERS * LEV
CHUNK = 4
CHUNKS = COLS // CHUNK
PAIRS = ROWS // 2
BLOCK = CHUNK * ROWS
SHARE = LEV // MEM


def nt(a, b):
    return lax.dot_general(a, b, (((1,), (1,)), ((), ())), preferred_element_type=jnp.float32)


def iota(shape, dim):
    return lax.broadcasted_iota(jnp.int32, shape, dim)


def positions_down(counts, slab, place, missing):
    rows = slab.shape[0]
    devices = iota((rows, GRID), 1)
    table = jnp.broadcast_to(counts, (128, GRID)).astype(jnp.bfloat16)
    start = nt((devices < slab).astype(jnp.float32).astype(jnp.bfloat16), table)
    count = nt((devices == slab).astype(jnp.float32).astype(jnp.bfloat16), table)
    place = place.astype(jnp.float32)
    return jnp.where(place < count, start + place, missing)


def positions_across(counts, slab, place, missing):
    lanes = slab.shape[1]
    devices = iota((GRID, lanes), 0)
    table = jnp.broadcast_to(counts, (8, GRID)).astype(jnp.bfloat16)
    before = (devices < slab).astype(jnp.float32).astype(jnp.bfloat16)
    own = (devices == slab).astype(jnp.float32).astype(jnp.bfloat16)
    start = jnp.dot(table, before, preferred_element_type=jnp.float32)
    count = jnp.dot(table, own, preferred_element_type=jnp.float32)
    place = place.astype(jnp.float32)
    return jnp.where(place < count, start + place, missing)


def weights(lag, inside):
    return jnp.where(inside, jnp.exp(lag * (-1.0 / LENGTH)) * SCALE, 0.0).astype(jnp.bfloat16)


def interleave(first, second):
    low = iota(first.shape, 1) < 4
    even = jnp.where(low, first, pltpu.roll(second, 4, 1))
    odd = jnp.where(low, pltpu.roll(first, 4, 1), second)
    return even, odd


def kernel(control, perturbation, vertical, lat_counts, lon_counts, out,
           ctrl, pert, vert, latc, lonc, lon_t, lat_k, send, recv, wide, part, parts,
           in_sem, send_sem, recv_sem, own_sem, psend_sem, precv_sem, pown_sem):
    me = lax.axis_index("grid")
    mine = lax.axis_index("mem")
    loads = [pltpu.make_async_copy(source, target, in_sem.at[index]) for index, (source, target) in enumerate(
        ((lon_counts, lonc), (lat_counts, latc), (vertical, vert), (control, ctrl), (perturbation, pert)))]
    for load in loads:
        load.start()

    barrier = pltpu.get_barrier_semaphore()

    def greet(step, carry):
        pl.semaphore_signal(barrier, inc=1, device_id={"grid": lax.rem(me + step, GRID)}, device_id_type=MESH)
        return carry

    lax.fori_loop(1, GRID, greet, 0)
    for step in range(1, MEM):
        pl.semaphore_signal(barrier, inc=1, device_id={"mem": lax.rem(mine + step, MEM)}, device_id_type=MESH)

    loads[0].wait()
    counts = lonc[...].astype(jnp.float32)
    lanes = iota((GRID, LON_PAD), 1)
    source = positions_across(counts, lanes // COLS, lanes[:8] % COLS, -FAR)
    for q in range(CHUNKS):
        rows = iota((GRID * CHUNK, GRID), 0)
        place = iota((GRID * CHUNK, 128), 0) % CHUNK + q * CHUNK
        target = positions_down(counts, rows // CHUNK, place, FAR)
        for tile in range(LON_PAD // 128):
            lag = target - source[:1, tile * 128:(tile + 1) * 128]
            lag = jnp.where(lag < 0, lag + LON, lag)
            lon_t[q, :, tile * 128:(tile + 1) * 128] = weights(lag, lag <= BAND)

    loads[3].wait()
    own = []
    for q in range(CHUNKS):
        fields = jnp.concatenate([ctrl[:, i].reshape(LANES, LON_PAD) for i in range(ROWS)], axis=0)
        smooth = nt(lon_t[q], fields)
        for pair in range(PAIRS):
            first, second = [smooth[:, (2 * pair + half) * LANES:(2 * pair + half + 1) * LANES].reshape(GRID * CHUNK // 8, 8, LANES)
                             for half in range(2)]
            even, odd = interleave(first, second)
            send[q, :, 0, pair * 8:(pair + 1) * 8, :] = even.astype(jnp.bfloat16)
            send[q, :, 1, pair * 8:(pair + 1) * 8, :] = odd.astype(jnp.bfloat16)
        if q == 0:
            pl.semaphore_wait(barrier, GRID - 1 + MEM - 1)

        def push(step, carry):
            peer = lax.rem(me + step, GRID)
            pltpu.make_async_remote_copy(
                src_ref=send.at[q, peer // 2, peer % 2], dst_ref=recv.at[q, me],
                send_sem=send_sem.at[q], recv_sem=recv_sem.at[q],
                device_id={"grid": peer}, device_id_type=MESH).start()
            return carry

        lax.fori_loop(1, GRID, push, 0)
        keep = pltpu.make_async_copy(send.at[q, me // 2, me % 2], recv.at[q, me], own_sem.at[q])
        keep.start()
        own.append(keep)

    loads[1].wait()
    counts = latc[...].astype(jnp.float32)
    half_rows = GRID * PAIRS
    lanes = iota((GRID, LAT_PAD), 1)
    target = positions_across(counts, lanes // ROWS, lanes[:8] % ROWS, -FAR)
    rows = iota((LAT_PAD, GRID), 0) % half_rows
    long_rows = iota((LAT_PAD, 128), 0)
    place = 2 * (long_rows % PAIRS) + long_rows // half_rows
    source = positions_down(counts, rows // PAIRS, place, FAR)
    for tile in range(LAT_PAD // 128):
        lag = target[:1, tile * 128:(tile + 1) * 128] - source
        lat_k[:, tile * 128:(tile + 1) * 128] = weights(lag, (lag >= 0) & (lag <= BAND))

    loads[2].wait()
    spread = (iota((LEV, LANES), 0) == iota((LEV, LANES), 1) % LEV).astype(jnp.float32).astype(jnp.bfloat16)
    across = jnp.dot(vert[...], spread, preferred_element_type=jnp.float32)
    across = jnp.concatenate([across] * MEMBERS, axis=0)
    mixing = jnp.where(iota((LANES, LANES), 0) // LEV == iota((LANES, LANES), 1) // LEV, across, 0.0).astype(jnp.bfloat16)

    loads[4].wait()
    for q in range(CHUNKS):
        own[q].wait()
        pltpu.make_async_copy(recv.at[q, pl.ds(0, GRID - 1)], recv.at[q, pl.ds(0, GRID - 1)], recv_sem.at[q]).wait()
        wide[...] = recv[q].astype(jnp.float32).reshape(GRID * BLOCK, LANES)
        mixed = []
        for c in range(CHUNK):
            fields = jnp.concatenate([wide[pl.ds(half * CHUNK + c, half_rows, stride=2 * CHUNK), :] for half in range(2)], axis=0)
            mixed.append(nt(mixing, fields.astype(jnp.bfloat16)).astype(jnp.bfloat16))
        filtered = jnp.dot(jnp.concatenate(mixed, axis=0), lat_k[...], preferred_element_type=jnp.float32)
        sums = []
        for c in range(CHUNK):
            field = filtered[c * LANES:(c + 1) * LANES].reshape(MEMBERS, LEV, LAT_PAD)
            sums.append(jnp.sum(field * pert[:, q * CHUNK + c].astype(jnp.float32), axis=0).reshape(LEV // 8, 8, LAT_PAD))
        for two in range(CHUNK // 2):
            even, odd = interleave(sums[2 * two], sums[2 * two + 1])
            part[q, :, 0, two * 8:(two + 1) * 8, :] = even.astype(jnp.bfloat16)
            part[q, :, 1, two * 8:(two + 1) * 8, :] = odd.astype(jnp.bfloat16)
        for step in range(1, MEM):
            peer = lax.rem(mine + step, MEM)
            pltpu.make_async_remote_copy(
                src_ref=part.at[q, peer // 2, peer % 2], dst_ref=parts.at[q, mine],
                send_sem=psend_sem.at[q], recv_sem=precv_sem.at[q],
                device_id={"mem": peer}, device_id_type=MESH).start()
        pltpu.make_async_copy(part.at[q, mine // 2, mine % 2], parts.at[q, mine], pown_sem.at[q]).start()

    rows = CHUNK * SHARE
    for q in range(CHUNKS):
        pltpu.make_async_copy(part.at[q, 0, 0], parts.at[q, 0], pown_sem.at[q]).wait()
        pltpu.make_async_copy(parts.at[q, pl.ds(0, MEM - 1)], parts.at[q, pl.ds(0, MEM - 1)], precv_sem.at[q]).wait()
        out[q * rows:(q + 1) * rows, :] = jnp.sum(parts[q].astype(jnp.float32), axis=0)
    for q in range(CHUNKS):
        pltpu.make_async_copy(recv.at[q, pl.ds(0, GRID - 1)], recv.at[q, pl.ds(0, GRID - 1)], send_sem.at[q]).wait()
        pltpu.make_async_copy(parts.at[q, pl.ds(0, MEM - 1)], parts.at[q, pl.ds(0, MEM - 1)], psend_sem.at[q]).wait()


def per_device(control, perturbation, vertical, lat_counts, lon_counts):
    bf16 = jnp.bfloat16
    dma = pltpu.SemaphoreType.DMA
    rows = CHUNK * SHARE
    summed = pl.pallas_call(
        kernel,
        out_shape=jax.ShapeDtypeStruct((COLS * SHARE, LAT_PAD), jnp.float32),
        in_specs=[pl.BlockSpec(memory_space=pltpu.HBM)] * 5,
        out_specs=pl.BlockSpec(memory_space=pltpu.VMEM),
        scratch_shapes=[
            pltpu.VMEM((MEMBERS, ROWS, LEV, LON_PAD), bf16),
            pltpu.VMEM((MEMBERS, COLS, LEV, LAT_PAD), bf16),
            pltpu.VMEM((LEV, LEV), bf16),
            pltpu.VMEM((1, GRID), jnp.int32),
            pltpu.VMEM((1, GRID), jnp.int32),
            pltpu.VMEM((CHUNKS, GRID * CHUNK, LON_PAD), bf16),
            pltpu.VMEM((LAT_PAD, LAT_PAD), bf16),
            pltpu.VMEM((CHUNKS, GRID // 2, 2, BLOCK, LANES), bf16),
            pltpu.VMEM((CHUNKS, GRID, BLOCK, LANES), bf16),
            pltpu.VMEM((GRID * BLOCK, LANES), jnp.float32),
            pltpu.VMEM((CHUNKS, MEM // 2, 2, rows, LAT_PAD), bf16),
            pltpu.VMEM((CHUNKS, MEM, rows, LAT_PAD), bf16),
            dma((5,)), dma((CHUNKS,)), dma((CHUNKS,)), dma((CHUNKS,)), dma((CHUNKS,)), dma((CHUNKS,)), dma((CHUNKS,)),
        ],
        compiler_params=pltpu.CompilerParams(collective_id=0, has_side_effects=True, vmem_limit_bytes=60 * 1024 * 1024),
    )(jnp.transpose(control, (0, 2, 1, 3)), jnp.transpose(perturbation, (0, 2, 1, 3)), vertical,
      lat_counts.reshape(1, GRID), lon_counts.reshape(1, GRID))
    return jnp.transpose(summed.reshape(COLS, SHARE, LAT_PAD), (1, 0, 2))


def solution(mesh):
    in_specs = (P("mem", None, "grid", None), P("mem", None, "grid", None), P(), P(), P())
    out_specs = P("mem", "grid", None)
    return jax.shard_map(
        per_device, mesh=mesh, in_specs=in_specs, out_specs=out_specs, check_vma=False
    )
```

time: 179 us -> 54.5 us (0.30)
  waiting for transfers between devices: 110 us -> 0 us
  Pallas kernels: 0 us -> 52.8 us
  local copies, waits for them, and re-layouts: 30 us -> 1.54 us
  between operations: 14.2 us -> 0.01 us
  starting transfers between devices: 13.1 us -> 0 us
  matrix products: 8.74 us -> 0 us
  other arithmetic: 2.63 us -> 0 us
    psum x1 -> x0, waiting for transfers between devices: 81.6 us -> none  [per_device(): summed = lax.psum(partial_value, 'mem')]
    pallas_call x0 -> x1, Pallas kernels: none -> 52.8 us  [per_device(): pl.pallas_call(kernel, out_shape=jax.ShapeDtypeStruct((COLS * SHARE, LAT_...]
    all_to_all x1 -> x0, waiting for transfers between devices: 28.2 us -> none  [per_device(): lax.all_to_all(smooth, 'grid', split_axis=3, concat_axis=2, tiled=True)]
    unnamed x9 -> x0, local copies, waits for them, and re-layouts: 14.2 us -> none
    all_to_all x1 -> x0, starting transfers between devices: 13.1 us -> none  [per_device(): lax.all_to_all(smooth, 'grid', split_axis=3, concat_axis=2, tiled=True)]
    dot_general x2 -> x0, matrix products: 8.74 us -> none  [the longest x1 5.89 us: per_device(): jnp.einsum('kl,mlci->mkci', vertical, filtered, preferred_element_type=jn...]
    all_to_all x1 -> x0, local copies, waits for them, and re-layouts: 6.17 us -> none  [per_device(): lax.all_to_all(smooth, 'grid', split_axis=3, concat_axis=2, tiled=True)]
    reshape x3 -> x1, local copies, waits for them, and re-layouts: 7.22 us -> 1.54 us  [per_device(): return jnp.transpose(summed.reshape(COLS, SHARE, LAT_PAD), (1, 0, 2))]
  transfers between devices with their start and end apart: 2 -> 0, of which waited for: 2 -> 0; matrix products, arithmetic and copies ran while one was open for 0% -> 0% of each run, Pallas kernels for 0% -> 0%
where the time goes in v1:
time: 54.5 us; the launch traced here: 54.3 us
  Pallas kernels  52.8 us (97%)
  local copies, waits for them, and re-layouts  1.54 us (3%)
    pallas_call x1, Pallas kernels, per_device(): pl.pallas_call(kernel, out_shape=jax.ShapeDtypeStruct((COLS * SHARE, LAT_...  52.8 us
    reshape x1, local copies, waits for them, and re-layouts, per_device(): return jnp.transpose(summed.reshape(COLS, SHARE, LAT_PAD), (1, 0, 2))  1.54 us

profile of v1, /device:TPU:1, one launch (start us, length us, event | category | flops | bytes accessed | tf_op | source)
XLA Modules:
  0.0 54.3 jit_solution(3335163963827800230)
XLA Ops:
  0.0 52.8 %shard_map.55 = f32[48,384]{1,0:T(8,128)} custom-call(bf16[4,6,32,768]{3,2,1,0:T(8,128)(2,1)} %bitcast.5, bf16[4,12,32,384]{3,2,1,0:T(8,128)(2,1)} %bitcast.6, bf16[32,32]{1,0:T(8,128)(2,1)} %vertical.1, s32[1,64]{1,0:T(1,128)} %bitcast.7, s32[1,64]{1,0:T(1,128)} %bitcast.8), custom_call_target="tpu_custom_call" | custom-call | tf_op jit(solution)/shard_map/pallas_call | solution.py:196
  52.8 1.5 %reshape.11 = f32[12,4,384]{2,1,0:T(4,128)} reshape(f32[48,384]{1,0:T(8,128)} %shard_map.55) | data formatting | bytes 147456 | tf_op jit(solution)/shard_map/reshape | solution.py:219

commit v2 on v1

--- a/solution.py
+++ b/solution.py
@@ -18,6 +18,7 @@
 SCALE = float(np.float32(1.0) / NORM)
 
 GRID = 64
+SIDE = 8
 MEM = 8
 MEMBERS = 4
 LEV = 32
@@ -31,6 +32,8 @@
 PAIRS = ROWS // 2
 BLOCK = CHUNK * ROWS
 SHARE = LEV // MEM
+TILE = 8
+PIECES = ((0, 0, 1), (0, 1, 2), (1, 0, 3), (2, 0, 3))
 
 
 def nt(a, b):
@@ -75,24 +78,34 @@
 
 
 def kernel(control, perturbation, vertical, lat_counts, lon_counts, out,
-           ctrl, pert, vert, latc, lonc, lon_t, lat_k, send, recv, wide, part, parts,
-           in_sem, send_sem, recv_sem, own_sem, psend_sem, precv_sem, pown_sem):
+           ctrl, pert, vert, latc, lonc, lon_t, lat_k, send, middle, recv, wide, part, parts,
+           in_sem, mid_send_sem, mid_recv_sem, send_sem, recv_sem, own_sem, near_sem, psend_sem, precv_sem, pown_sem):
     me = lax.axis_index("grid")
     mine = lax.axis_index("mem")
+    my_y, my_x, my_z = me // SIDE, (me % SIDE) // 2, me % 2
+
+    def across(step):
+        to_x, to_z = (my_x + step // 2) % 4, (my_z + step % 2) % 2
+        return my_y * SIDE + to_x * 2 + to_z, to_x, to_z
+
+    def along(step):
+        to_y = (my_y + step) % SIDE
+        return to_y * SIDE + me % SIDE, to_y
+
     loads = [pltpu.make_async_copy(source, target, in_sem.at[index]) for index, (source, target) in enumerate(
-        ((lon_counts, lonc), (lat_counts, latc), (vertical, vert), (control, ctrl), (perturbation, pert)))]
+        ((lon_counts, lonc), (control, ctrl), (lat_counts, latc), (vertical, vert), (perturbation, pert)))]
     for load in loads:
         load.start()
 
     barrier = pltpu.get_barrier_semaphore()
 
     def greet(step, carry):
-        pl.semaphore_signal(barrier, inc=1, device_id={"grid": lax.rem(me + step, GRID)}, device_id_type=MESH)
+        pl.semaphore_signal(barrier, inc=1, device_id={"grid": across(step)[0]}, device_id_type=MESH)
+        pl.semaphore_signal(barrier, inc=1, device_id={"grid": along(step)[0]}, device_id_type=MESH)
+        pl.semaphore_signal(barrier, inc=1, device_id={"mem": (mine + step) % MEM}, device_id_type=MESH)
         return carry
 
-    lax.fori_loop(1, GRID, greet, 0)
-    for step in range(1, MEM):
-        pl.semaphore_signal(barrier, inc=1, device_id={"mem": lax.rem(mine + step, MEM)}, device_id_type=MESH)
+    lax.fori_loop(1, SIDE, greet, 0)
 
     loads[0].wait()
     counts = lonc[...].astype(jnp.float32)
@@ -106,57 +119,93 @@
             lag = target - source[:1, tile * 128:(tile + 1) * 128]
             lag = jnp.where(lag < 0, lag + LON, lag)
             lon_t[q, :, tile * 128:(tile + 1) * 128] = weights(lag, lag <= BAND)
-
-    loads[3].wait()
-    own = []
-    for q in range(CHUNKS):
+        if q == 0:
+            loads[1].wait()
         fields = jnp.concatenate([ctrl[:, i].reshape(LANES, LON_PAD) for i in range(ROWS)], axis=0)
         smooth = nt(lon_t[q], fields)
         for pair in range(PAIRS):
             first, second = [smooth[:, (2 * pair + half) * LANES:(2 * pair + half + 1) * LANES].reshape(GRID * CHUNK // 8, 8, LANES)
                              for half in range(2)]
-            even, odd = interleave(first, second)
-            send[q, :, 0, pair * 8:(pair + 1) * 8, :] = even.astype(jnp.bfloat16)
-            send[q, :, 1, pair * 8:(pair + 1) * 8, :] = odd.astype(jnp.bfloat16)
+            for parity, block in enumerate(interleave(first, second)):
+                send[q, :, :, parity, pair * TILE:(pair + 1) * TILE, :] = block.astype(jnp.bfloat16).reshape(SIDE, 4, TILE, LANES)
         if q == 0:
-            pl.semaphore_wait(barrier, GRID - 1 + MEM - 1)
-
-        def push(step, carry):
-            peer = lax.rem(me + step, GRID)
+            pl.semaphore_wait(barrier, 3 * (SIDE - 1))
+
+        def direct(step, carry):
+            peer, to_y = along(step)
             pltpu.make_async_remote_copy(
-                src_ref=send.at[q, peer // 2, peer % 2], dst_ref=recv.at[q, me],
+                src_ref=send.at[q, to_y, my_x, my_z], dst_ref=recv.at[q, my_y, 0],
                 send_sem=send_sem.at[q], recv_sem=recv_sem.at[q],
                 device_id={"grid": peer}, device_id_type=MESH).start()
             return carry
 
-        lax.fori_loop(1, GRID, push, 0)
-        keep = pltpu.make_async_copy(send.at[q, me // 2, me % 2], recv.at[q, me], own_sem.at[q])
-        keep.start()
-        own.append(keep)
-
-    loads[1].wait()
+        lax.fori_loop(1, SIDE, direct, 0)
+        for piece, (chunk, group, groups) in enumerate(PIECES):
+            if chunk != q:
+                continue
+            span = pl.ds(group * TILE, groups * TILE)
+
+            def spread(step, carry):
+                peer, to_x, to_z = across(step)
+                pltpu.make_async_remote_copy(
+                    src_ref=send.at[q, :, to_x, to_z, span], dst_ref=middle.at[q, step - 1, :, span],
+                    send_sem=mid_send_sem.at[piece], recv_sem=mid_recv_sem.at[piece],
+                    device_id={"grid": peer}, device_id_type=MESH).start()
+                return carry
+
+            lax.fori_loop(1, SIDE, spread, 0)
+        pltpu.make_async_copy(send.at[q, my_y, my_x, my_z], recv.at[q, my_y, 0], own_sem.at[q]).start()
+
+    def pass_on(piece):
+        q, group, groups = PIECES[piece]
+        span = pl.ds(group * TILE, groups * TILE)
+        pltpu.make_async_copy(middle.at[q, :, :, span], middle.at[q, :, :, span], mid_recv_sem.at[piece]).wait()
+
+        def forward(step, carry):
+            peer, to_y = along(step)
+            pltpu.make_async_remote_copy(
+                src_ref=middle.at[q, :, to_y, span], dst_ref=recv.at[q, my_y, pl.ds(1, SIDE - 1), span],
+                send_sem=send_sem.at[q], recv_sem=recv_sem.at[q],
+                device_id={"grid": peer}, device_id_type=MESH).start()
+            return carry
+
+        lax.fori_loop(1, SIDE, forward, 0)
+        pltpu.make_async_copy(middle.at[q, :, my_y, span], recv.at[q, my_y, pl.ds(1, SIDE - 1), span], near_sem.at[piece]).start()
+
+    pass_on(0)
+
+    loads[2].wait()
     counts = latc[...].astype(jnp.float32)
     half_rows = GRID * PAIRS
     lanes = iota((GRID, LAT_PAD), 1)
     target = positions_across(counts, lanes // ROWS, lanes[:8] % ROWS, -FAR)
-    rows = iota((LAT_PAD, GRID), 0) % half_rows
+    block = iota((LAT_PAD, GRID), 0) % half_rows // PAIRS
+    step = block % SIDE
+    slab = block // SIDE * SIDE + (my_x + 4 - step // 2) % 4 * 2 + (my_z + 2 - step % 2) % 2
     long_rows = iota((LAT_PAD, 128), 0)
     place = 2 * (long_rows % PAIRS) + long_rows // half_rows
-    source = positions_down(counts, rows // PAIRS, place, FAR)
+    source = positions_down(counts, slab, place, FAR)
     for tile in range(LAT_PAD // 128):
         lag = target[:1, tile * 128:(tile + 1) * 128] - source
         lat_k[:, tile * 128:(tile + 1) * 128] = weights(lag, (lag >= 0) & (lag <= BAND))
 
-    loads[2].wait()
-    spread = (iota((LEV, LANES), 0) == iota((LEV, LANES), 1) % LEV).astype(jnp.float32).astype(jnp.bfloat16)
-    across = jnp.dot(vert[...], spread, preferred_element_type=jnp.float32)
-    across = jnp.concatenate([across] * MEMBERS, axis=0)
-    mixing = jnp.where(iota((LANES, LANES), 0) // LEV == iota((LANES, LANES), 1) // LEV, across, 0.0).astype(jnp.bfloat16)
+    loads[3].wait()
+    spread_lanes = (iota((LEV, LANES), 0) == iota((LEV, LANES), 1) % LEV).astype(jnp.float32).astype(jnp.bfloat16)
+    wide_factor = jnp.dot(vert[...], spread_lanes, preferred_element_type=jnp.float32)
+    wide_factor = jnp.concatenate([wide_factor] * MEMBERS, axis=0)
+    mixing = jnp.where(iota((LANES, LANES), 0) // LEV == iota((LANES, LANES), 1) // LEV, wide_factor, 0.0).astype(jnp.bfloat16)
+
+    for piece in range(1, len(PIECES)):
+        pass_on(piece)
 
     loads[4].wait()
     for q in range(CHUNKS):
-        own[q].wait()
-        pltpu.make_async_copy(recv.at[q, pl.ds(0, GRID - 1)], recv.at[q, pl.ds(0, GRID - 1)], recv_sem.at[q]).wait()
+        pltpu.make_async_copy(send.at[q, my_y, my_x, my_z], recv.at[q, my_y, 0], own_sem.at[q]).wait()
+        for piece, (chunk, group, groups) in enumerate(PIECES):
+            if chunk == q:
+                span = pl.ds(group * TILE, groups * TILE)
+                pltpu.make_async_copy(middle.at[q, :, my_y, span], recv.at[q, my_y, pl.ds(1, SIDE - 1), span], near_sem.at[piece]).wait()
+        pltpu.make_async_copy(recv.at[q, pl.ds(0, SIDE - 1)], recv.at[q, pl.ds(0, SIDE - 1)], recv_sem.at[q]).wait()
         wide[...] = recv[q].astype(jnp.float32).reshape(GRID * BLOCK, LANES)
         mixed = []
         for c in range(CHUNK):
@@ -168,11 +217,10 @@
             field = filtered[c * LANES:(c + 1) * LANES].reshape(MEMBERS, LEV, LAT_PAD)
             sums.append(jnp.sum(field * pert[:, q * CHUNK + c].astype(jnp.float32), axis=0).reshape(LEV // 8, 8, LAT_PAD))
         for two in range(CHUNK // 2):
-            even, odd = interleave(sums[2 * two], sums[2 * two + 1])
-            part[q, :, 0, two * 8:(two + 1) * 8, :] = even.astype(jnp.bfloat16)
-            part[q, :, 1, two * 8:(two + 1) * 8, :] = odd.astype(jnp.bfloat16)
+            for parity, block in enumerate(interleave(sums[2 * two], sums[2 * two + 1])):
+                part[q, :, parity, two * TILE:(two + 1) * TILE, :] = block.astype(jnp.bfloat16)
         for step in range(1, MEM):
-            peer = lax.rem(mine + step, MEM)
+            peer = (mine + step) % MEM
             pltpu.make_async_remote_copy(
                 src_ref=part.at[q, peer // 2, peer % 2], dst_ref=parts.at[q, mine],
                 send_sem=psend_sem.at[q], recv_sem=precv_sem.at[q],
@@ -181,11 +229,14 @@
 
     rows = CHUNK * SHARE
     for q in range(CHUNKS):
-        pltpu.make_async_copy(part.at[q, 0, 0], parts.at[q, 0], pown_sem.at[q]).wait()
+        pltpu.make_async_copy(part.at[q, mine // 2, mine % 2], parts.at[q, mine], pown_sem.at[q]).wait()
         pltpu.make_async_copy(parts.at[q, pl.ds(0, MEM - 1)], parts.at[q, pl.ds(0, MEM - 1)], precv_sem.at[q]).wait()
         out[q * rows:(q + 1) * rows, :] = jnp.sum(parts[q].astype(jnp.float32), axis=0)
-    for q in range(CHUNKS):
-        pltpu.make_async_copy(recv.at[q, pl.ds(0, GRID - 1)], recv.at[q, pl.ds(0, GRID - 1)], send_sem.at[q]).wait()
+    for piece, (q, group, groups) in enumerate(PIECES):
+        span = pl.ds(group * TILE, groups * TILE)
+        pltpu.make_async_copy(middle.at[q, :, :, span], middle.at[q, :, :, span], mid_send_sem.at[piece]).wait()
+    for q in range(CHUNKS):
+        pltpu.make_async_copy(recv.at[q, pl.ds(0, SIDE - 1)], recv.at[q, pl.ds(0, SIDE - 1)], send_sem.at[q]).wait()
         pltpu.make_async_copy(parts.at[q, pl.ds(0, MEM - 1)], parts.at[q, pl.ds(0, MEM - 1)], psend_sem.at[q]).wait()
 
 
@@ -206,12 +257,14 @@
             pltpu.VMEM((1, GRID), jnp.int32),
             pltpu.VMEM((CHUNKS, GRID * CHUNK, LON_PAD), bf16),
             pltpu.VMEM((LAT_PAD, LAT_PAD), bf16),
-            pltpu.VMEM((CHUNKS, GRID // 2, 2, BLOCK, LANES), bf16),
-            pltpu.VMEM((CHUNKS, GRID, BLOCK, LANES), bf16),
+            pltpu.VMEM((CHUNKS, SIDE, 4, 2, BLOCK, LANES), bf16),
+            pltpu.VMEM((CHUNKS, SIDE - 1, SIDE, BLOCK, LANES), bf16),
+            pltpu.VMEM((CHUNKS, SIDE, SIDE, BLOCK, LANES), bf16),
             pltpu.VMEM((GRID * BLOCK, LANES), jnp.float32),
             pltpu.VMEM((CHUNKS, MEM // 2, 2, rows, LAT_PAD), bf16),
             pltpu.VMEM((CHUNKS, MEM, rows, LAT_PAD), bf16),
-            dma((5,)), dma((CHUNKS,)), dma((CHUNKS,)), dma((CHUNKS,)), dma((CHUNKS,)), dma((CHUNKS,)), dma((CHUNKS,)),
+            dma((5,)), dma((len(PIECES),)), dma((len(PIECES),)), dma((CHUNKS,)), dma((CHUNKS,)), dma((CHUNKS,)),
+            dma((len(PIECES),)), dma((CHUNKS,)), dma((CHUNKS,)), dma((CHUNKS,)),
         ],
         compiler_params=pltpu.CompilerParams(collective_id=0, has_side_effects=True, vmem_limit_bytes=60 * 1024 * 1024),
     )(jnp.transpose(control, (0, 2, 1, 3)), jnp.transpose(perturbation, (0, 2, 1, 3)), vertical,

time: 54.5 us -> 53.1 us (0.974)
  Pallas kernels: 52.8 us -> 51.4 us
    pallas_call x1, Pallas kernels: 52.8 us -> 51.4 us  [per_device(): pl.pallas_call(kernel, out_shape=jax.ShapeDtypeStruct((COLS * SHARE, LAT_...]
where the time goes in v2:
time: 53.1 us; the launch traced here: 53 us
  Pallas kernels  51.4 us (97%)
  local copies, waits for them, and re-layouts  1.54 us (3%)
    pallas_call x1, Pallas kernels, per_device(): pl.pallas_call(kernel, out_shape=jax.ShapeDtypeStruct((COLS * SHARE, LAT_...  51.4 us
    reshape x1, local copies, waits for them, and re-layouts, per_device(): return jnp.transpose(summed.reshape(COLS, SHARE, LAT_PAD), (1, 0, 2))  1.54 us

profile of v2, /device:TPU:1, one launch (start us, length us, event | category | flops | bytes accessed | tf_op | source)
XLA Modules:
  0.0 53.0 jit_solution(9887411415524401122)
XLA Ops:
  0.0 51.4 %shard_map.55 = f32[48,384]{1,0:T(8,128)} custom-call(bf16[4,6,32,768]{3,2,1,0:T(8,128)(2,1)} %bitcast.5, bf16[4,12,32,384]{3,2,1,0:T(8,128)(2,1)} %bitcast.6, bf16[32,32]{1,0:T(8,128)(2,1)} %vertical.1, s32[1,64]{1,0:T(1,128)} %bitcast.7, s32[1,64]{1,0:T(1,128)} %bitcast.8), custom_call_target="tpu_custom_call" | custom-call | tf_op jit(solution)/shard_map/pallas_call | solution.py:247
  51.4 1.5 %reshape.11 = f32[12,4,384]{2,1,0:T(4,128)} reshape(f32[48,384]{1,0:T(8,128)} %shard_map.55) | data formatting | bytes 147456 | tf_op jit(solution)/shard_map/reshape | solution.py:272

commit v3 on v2

--- a/solution.py
+++ b/solution.py
@@ -89,13 +89,8 @@
         return my_y * SIDE + to_x * 2 + to_z, to_x, to_z
 
     def along(step):
-        to_y = (my_y + step) % SIDE
+        to_y = (my_y + 4 + (step // 2) * (2 * (step % 2) - 1)) % SIDE
         return to_y * SIDE + me % SIDE, to_y
-
-    loads = [pltpu.make_async_copy(source, target, in_sem.at[index]) for index, (source, target) in enumerate(
-        ((lon_counts, lonc), (control, ctrl), (lat_counts, latc), (vertical, vert), (perturbation, pert)))]
-    for load in loads:
-        load.start()
 
     barrier = pltpu.get_barrier_semaphore()
 
@@ -107,11 +102,16 @@
 
     lax.fori_loop(1, SIDE, greet, 0)
 
+    loads = [pltpu.make_async_copy(source, target, in_sem.at[index]) for index, (source, target) in enumerate(
+        ((lon_counts, lonc), (control, ctrl), (lat_counts, latc), (vertical, vert), (perturbation, pert)))]
+    for load in loads:
+        load.start()
+
     loads[0].wait()
     counts = lonc[...].astype(jnp.float32)
     lanes = iota((GRID, LON_PAD), 1)
     source = positions_across(counts, lanes // COLS, lanes[:8] % COLS, -FAR)
-    for q in range(CHUNKS):
+    def smooth_chunk(q):
         rows = iota((GRID * CHUNK, GRID), 0)
         place = iota((GRID * CHUNK, 128), 0) % CHUNK + q * CHUNK
         target = positions_down(counts, rows // CHUNK, place, FAR)
@@ -128,9 +128,8 @@
                              for half in range(2)]
             for parity, block in enumerate(interleave(first, second)):
                 send[q, :, :, parity, pair * TILE:(pair + 1) * TILE, :] = block.astype(jnp.bfloat16).reshape(SIDE, 4, TILE, LANES)
-        if q == 0:
-            pl.semaphore_wait(barrier, 3 * (SIDE - 1))
-
+
+    def send_direct(q):
         def direct(step, carry):
             peer, to_y = along(step)
             pltpu.make_async_remote_copy(
@@ -140,20 +139,22 @@
             return carry
 
         lax.fori_loop(1, SIDE, direct, 0)
-        for piece, (chunk, group, groups) in enumerate(PIECES):
-            if chunk != q:
-                continue
-            span = pl.ds(group * TILE, groups * TILE)
-
-            def spread(step, carry):
-                peer, to_x, to_z = across(step)
-                pltpu.make_async_remote_copy(
-                    src_ref=send.at[q, :, to_x, to_z, span], dst_ref=middle.at[q, step - 1, :, span],
-                    send_sem=mid_send_sem.at[piece], recv_sem=mid_recv_sem.at[piece],
-                    device_id={"grid": peer}, device_id_type=MESH).start()
-                return carry
-
-            lax.fori_loop(1, SIDE, spread, 0)
+
+    def send_piece(piece):
+        q, group, groups = PIECES[piece]
+        span = pl.ds(group * TILE, groups * TILE)
+
+        def spread(step, carry):
+            peer, to_x, to_z = across(step)
+            pltpu.make_async_remote_copy(
+                src_ref=send.at[q, :, to_x, to_z, span], dst_ref=middle.at[q, step - 1, :, span],
+                send_sem=mid_send_sem.at[piece], recv_sem=mid_recv_sem.at[piece],
+                device_id={"grid": peer}, device_id_type=MESH).start()
+            return carry
+
+        lax.fori_loop(1, SIDE, spread, 0)
+
+    def keep(q):
         pltpu.make_async_copy(send.at[q, my_y, my_x, my_z], recv.at[q, my_y, 0], own_sem.at[q]).start()
 
     def pass_on(piece):
@@ -172,7 +173,21 @@
         lax.fori_loop(1, SIDE, forward, 0)
         pltpu.make_async_copy(middle.at[q, :, my_y, span], recv.at[q, my_y, pl.ds(1, SIDE - 1), span], near_sem.at[piece]).start()
 
+    smooth_chunk(0)
+    pl.semaphore_wait(barrier, 3 * (SIDE - 1))
+    send_piece(0)
+    send_direct(0)
+    send_piece(1)
+    smooth_chunk(1)
+    send_direct(1)
+    send_piece(2)
+    smooth_chunk(2)
     pass_on(0)
+    send_direct(2)
+    send_piece(3)
+    for q in range(CHUNKS):
+        keep(q)
+    pass_on(1)
 
     loads[2].wait()
     counts = latc[...].astype(jnp.float32)
@@ -195,7 +210,7 @@
     wide_factor = jnp.concatenate([wide_factor] * MEMBERS, axis=0)
     mixing = jnp.where(iota((LANES, LANES), 0) // LEV == iota((LANES, LANES), 1) // LEV, wide_factor, 0.0).astype(jnp.bfloat16)
 
-    for piece in range(1, len(PIECES)):
+    for piece in range(2, len(PIECES)):
         pass_on(piece)
 
     loads[4].wait()

time: 53.1 us -> 52.3 us (0.985)
  Pallas kernels: 51.4 us -> 50.5 us
    pallas_call x1, Pallas kernels: 51.4 us -> 50.5 us  [per_device(): pl.pallas_call(kernel, out_shape=jax.ShapeDtypeStruct((COLS * SHARE, LAT_...]
where the time goes in v3:
time: 52.3 us; the launch traced here: 52.1 us
  Pallas kernels  50.5 us (97%)
  local copies, waits for them, and re-layouts  1.54 us (3%)
    pallas_call x1, Pallas kernels, per_device(): pl.pallas_call(kernel, out_shape=jax.ShapeDtypeStruct((COLS * SHARE, LAT_...  50.5 us
    reshape x1, local copies, waits for them, and re-layouts, per_device(): return jnp.transpose(summed.reshape(COLS, SHARE, LAT_PAD), (1, 0, 2))  1.54 us

profile of v3, /device:TPU:1, one launch (start us, length us, event | category | flops | bytes accessed | tf_op | source)
XLA Modules:
  0.0 52.1 jit_solution(9103716154852732735)
XLA Ops:
  0.0 50.5 %shard_map.55 = f32[48,384]{1,0:T(8,128)} custom-call(bf16[4,6,32,768]{3,2,1,0:T(8,128)(2,1)} %bitcast.5, bf16[4,12,32,384]{3,2,1,0:T(8,128)(2,1)} %bitcast.6, bf16[32,32]{1,0:T(8,128)(2,1)} %vertical.1, s32[1,64]{1,0:T(1,128)} %bitcast.7, s32[1,64]{1,0:T(1,128)} %bitcast.8), custom_call_target="tpu_custom_call" | custom-call | tf_op jit(solution)/shard_map/pallas_call | solution.py:262
  50.5 1.5 %reshape.11 = f32[12,4,384]{2,1,0:T(4,128)} reshape(f32[48,384]{1,0:T(8,128)} %shard_map.55) | data formatting | bytes 147456 | tf_op jit(solution)/shard_map/reshape | solution.py:287

commit v4 on v3

--- a/solution.py
+++ b/solution.py
@@ -33,7 +33,7 @@
 BLOCK = CHUNK * ROWS
 SHARE = LEV // MEM
 TILE = 8
-PIECES = ((0, 0, 1), (0, 1, 2), (1, 0, 3), (2, 0, 3))
+PIECES = ((1, 0, 3), (2, 0, 3))
 
 
 def nt(a, b):
@@ -78,8 +78,8 @@
 
 
 def kernel(control, perturbation, vertical, lat_counts, lon_counts, out,
-           ctrl, pert, vert, latc, lonc, lon_t, lat_k, send, middle, recv, wide, part, parts,
-           in_sem, mid_send_sem, mid_recv_sem, send_sem, recv_sem, own_sem, near_sem, psend_sem, precv_sem, pown_sem):
+           ctrl, pert, vert, latc, lonc, lon_t, lat_k, send, column, middle, recv, wide, part, parts,
+           in_sem, mid_send_sem, mid_recv_sem, send_sem, recv_sem, own_sem, near_sem, psend_sem, precv_sem, pown_sem, col_send_sem, col_recv_sem, col_own_sem):
     me = lax.axis_index("grid")
     mine = lax.axis_index("mem")
     my_y, my_x, my_z = me // SIDE, (me % SIDE) // 2, me % 2
@@ -140,6 +140,36 @@
 
         lax.fori_loop(1, SIDE, direct, 0)
 
+    stay = pltpu.make_async_copy(send.at[0, my_y], column.at[my_y], own_sem.at[0])
+    settle = pltpu.make_async_copy(column.at[:, my_x, my_z], recv.at[0, :, 0], col_own_sem.at[0])
+
+    def send_column():
+        def far(step, carry):
+            peer, to_y = along(step)
+            pltpu.make_async_remote_copy(
+                src_ref=send.at[0, to_y], dst_ref=column.at[my_y],
+                send_sem=col_send_sem.at[0], recv_sem=col_recv_sem.at[0],
+                device_id={"grid": peer}, device_id_type=MESH).start()
+            return carry
+
+        lax.fori_loop(1, SIDE, far, 0)
+        stay.start()
+
+    def pass_column():
+        stay.wait()
+        pltpu.make_async_copy(column.at[pl.ds(0, SIDE - 1)], column.at[pl.ds(0, SIDE - 1)], col_recv_sem.at[0]).wait()
+
+        def near(step, carry):
+            peer, to_x, to_z = across(step)
+            pltpu.make_async_remote_copy(
+                src_ref=column.at[:, to_x, to_z], dst_ref=recv.at[0, :, step],
+                send_sem=send_sem.at[0], recv_sem=recv_sem.at[0],
+                device_id={"grid": peer}, device_id_type=MESH).start()
+            return carry
+
+        lax.fori_loop(1, SIDE, near, 0)
+        settle.start()
+
     def send_piece(piece):
         q, group, groups = PIECES[piece]
         span = pl.ds(group * TILE, groups * TILE)
@@ -175,19 +205,15 @@
 
     smooth_chunk(0)
     pl.semaphore_wait(barrier, 3 * (SIDE - 1))
+    send_column()
+    smooth_chunk(1)
     send_piece(0)
-    send_direct(0)
+    send_direct(1)
+    smooth_chunk(2)
     send_piece(1)
-    smooth_chunk(1)
-    send_direct(1)
-    send_piece(2)
-    smooth_chunk(2)
-    pass_on(0)
     send_direct(2)
-    send_piece(3)
-    for q in range(CHUNKS):
+    for q in range(1, CHUNKS):
         keep(q)
-    pass_on(1)
 
     loads[2].wait()
     counts = latc[...].astype(jnp.float32)
@@ -210,12 +236,16 @@
     wide_factor = jnp.concatenate([wide_factor] * MEMBERS, axis=0)
     mixing = jnp.where(iota((LANES, LANES), 0) // LEV == iota((LANES, LANES), 1) // LEV, wide_factor, 0.0).astype(jnp.bfloat16)
 
-    for piece in range(2, len(PIECES)):
-        pass_on(piece)
+    pass_on(0)
+    pass_column()
+    pass_on(1)
 
     loads[4].wait()
     for q in range(CHUNKS):
-        pltpu.make_async_copy(send.at[q, my_y, my_x, my_z], recv.at[q, my_y, 0], own_sem.at[q]).wait()
+        if q == 0:
+            settle.wait()
+        else:
+            pltpu.make_async_copy(send.at[q, my_y, my_x, my_z], recv.at[q, my_y, 0], own_sem.at[q]).wait()
         for piece, (chunk, group, groups) in enumerate(PIECES):
             if chunk == q:
                 span = pl.ds(group * TILE, groups * TILE)
@@ -247,6 +277,7 @@
         pltpu.make_async_copy(part.at[q, mine // 2, mine % 2], parts.at[q, mine], pown_sem.at[q]).wait()
         pltpu.make_async_copy(parts.at[q, pl.ds(0, MEM - 1)], parts.at[q, pl.ds(0, MEM - 1)], precv_sem.at[q]).wait()
         out[q * rows:(q + 1) * rows, :] = jnp.sum(parts[q].astype(jnp.float32), axis=0)
+    pltpu.make_async_copy(column.at[pl.ds(0, SIDE - 1)], column.at[pl.ds(0, SIDE - 1)], col_send_sem.at[0]).wait()
     for piece, (q, group, groups) in enumerate(PIECES):
         span = pl.ds(group * TILE, groups * TILE)
         pltpu.make_async_copy(middle.at[q, :, :, span], middle.at[q, :, :, span], mid_send_sem.at[piece]).wait()
@@ -273,13 +304,14 @@
             pltpu.VMEM((CHUNKS, GRID * CHUNK, LON_PAD), bf16),
             pltpu.VMEM((LAT_PAD, LAT_PAD), bf16),
             pltpu.VMEM((CHUNKS, SIDE, 4, 2, BLOCK, LANES), bf16),
+            pltpu.VMEM((SIDE, 4, 2, BLOCK, LANES), bf16),
             pltpu.VMEM((CHUNKS, SIDE - 1, SIDE, BLOCK, LANES), bf16),
             pltpu.VMEM((CHUNKS, SIDE, SIDE, BLOCK, LANES), bf16),
             pltpu.VMEM((GRID * BLOCK, LANES), jnp.float32),
             pltpu.VMEM((CHUNKS, MEM // 2, 2, rows, LAT_PAD), bf16),
             pltpu.VMEM((CHUNKS, MEM, rows, LAT_PAD), bf16),
             dma((5,)), dma((len(PIECES),)), dma((len(PIECES),)), dma((CHUNKS,)), dma((CHUNKS,)), dma((CHUNKS,)),
-            dma((len(PIECES),)), dma((CHUNKS,)), dma((CHUNKS,)), dma((CHUNKS,)),
+            dma((len(PIECES),)), dma((CHUNKS,)), dma((CHUNKS,)), dma((CHUNKS,)), dma((1,)), dma((1,)), dma((1,)),
         ],
         compiler_params=pltpu.CompilerParams(collective_id=0, has_side_effects=True, vmem_limit_bytes=60 * 1024 * 1024),
     )(jnp.transpose(control, (0, 2, 1, 3)), jnp.transpose(perturbation, (0, 2, 1, 3)), vertical,

time: 52.3 us -> 49.4 us (0.945)
  Pallas kernels: 50.5 us -> 47.6 us
    pallas_call x1, Pallas kernels: 50.5 us -> 47.6 us  [per_device(): pl.pallas_call(kernel, out_shape=jax.ShapeDtypeStruct((COLS * SHARE, LAT_...]
where the time goes in v4:
time: 49.4 us; the launch traced here: 49.2 us
  Pallas kernels  47.6 us (96%)
  local copies, waits for them, and re-layouts  1.54 us (3%)
    pallas_call x1, Pallas kernels, per_device(): pl.pallas_call(kernel, out_shape=jax.ShapeDtypeStruct((COLS * SHARE, LAT_...  47.6 us
    reshape x1, local copies, waits for them, and re-layouts, per_device(): return jnp.transpose(summed.reshape(COLS, SHARE, LAT_PAD), (1, 0, 2))  1.54 us

profile of v4, /device:TPU:1, one launch (start us, length us, event | category | flops | bytes accessed | tf_op | source)
XLA Modules:
  0.0 49.2 jit_solution(14925850399358457226)
XLA Ops:
  0.0 47.6 %shard_map.55 = f32[48,384]{1,0:T(8,128)} custom-call(bf16[4,6,32,768]{3,2,1,0:T(8,128)(2,1)} %bitcast.5, bf16[4,12,32,384]{3,2,1,0:T(8,128)(2,1)} %bitcast.6, bf16[32,32]{1,0:T(8,128)(2,1)} %vertical.1, s32[1,64]{1,0:T(1,128)} %bitcast.7, s32[1,64]{1,0:T(1,128)} %bitcast.8), custom_call_target="tpu_custom_call" | custom-call | tf_op jit(solution)/shard_map/pallas_call | solution.py:293
  47.7 1.5 %reshape.11 = f32[12,4,384]{2,1,0:T(4,128)} reshape(f32[48,384]{1,0:T(8,128)} %shard_map.55) | data formatting | bytes 147456 | tf_op jit(solution)/shard_map/reshape | solution.py:319

commit v5 on v4

--- a/solution.py
+++ b/solution.py
@@ -77,8 +77,8 @@
     return even, odd
 
 
-def kernel(control, perturbation, vertical, lat_counts, lon_counts, out,
-           ctrl, pert, vert, latc, lonc, lon_t, lat_k, send, column, middle, recv, wide, part, parts,
+def kernel(control, perturbation, vertical, lat_counts, lon_counts, parts,
+           ctrl, pert, vert, latc, lonc, lon_t, lat_k, send, column, middle, recv, wide, part,
            in_sem, mid_send_sem, mid_recv_sem, send_sem, recv_sem, own_sem, near_sem, psend_sem, precv_sem, pown_sem, col_send_sem, col_recv_sem, col_own_sem):
     me = lax.axis_index("grid")
     mine = lax.axis_index("mem")
@@ -261,40 +261,38 @@
         for c in range(CHUNK):
             field = filtered[c * LANES:(c + 1) * LANES].reshape(MEMBERS, LEV, LAT_PAD)
             sums.append(jnp.sum(field * pert[:, q * CHUNK + c].astype(jnp.float32), axis=0).reshape(LEV // 8, 8, LAT_PAD))
-        for two in range(CHUNK // 2):
-            for parity, block in enumerate(interleave(sums[2 * two], sums[2 * two + 1])):
-                part[q, :, parity, two * TILE:(two + 1) * TILE, :] = block.astype(jnp.bfloat16)
-        for step in range(1, MEM):
+        for c in range(CHUNK):
+            part[q, :, :, c] = sums[c].reshape(MEM // 2, 2, SHARE, LAT_PAD).astype(jnp.bfloat16)
+        span = pl.ds(q * CHUNK, CHUNK)
+        for step in (4, 3, 5, 2, 6, 1, 7):
             peer = (mine + step) % MEM
             pltpu.make_async_remote_copy(
-                src_ref=part.at[q, peer // 2, peer % 2], dst_ref=parts.at[q, mine],
+                src_ref=part.at[q, peer // 2, peer % 2], dst_ref=parts.at[mine, span],
                 send_sem=psend_sem.at[q], recv_sem=precv_sem.at[q],
                 device_id={"mem": peer}, device_id_type=MESH).start()
-        pltpu.make_async_copy(part.at[q, mine // 2, mine % 2], parts.at[q, mine], pown_sem.at[q]).start()
-
-    rows = CHUNK * SHARE
-    for q in range(CHUNKS):
-        pltpu.make_async_copy(part.at[q, mine // 2, mine % 2], parts.at[q, mine], pown_sem.at[q]).wait()
-        pltpu.make_async_copy(parts.at[q, pl.ds(0, MEM - 1)], parts.at[q, pl.ds(0, MEM - 1)], precv_sem.at[q]).wait()
-        out[q * rows:(q + 1) * rows, :] = jnp.sum(parts[q].astype(jnp.float32), axis=0)
+        pltpu.make_async_copy(part.at[q, mine // 2, mine % 2], parts.at[mine, span], pown_sem.at[q]).start()
+
     pltpu.make_async_copy(column.at[pl.ds(0, SIDE - 1)], column.at[pl.ds(0, SIDE - 1)], col_send_sem.at[0]).wait()
     for piece, (q, group, groups) in enumerate(PIECES):
         span = pl.ds(group * TILE, groups * TILE)
         pltpu.make_async_copy(middle.at[q, :, :, span], middle.at[q, :, :, span], mid_send_sem.at[piece]).wait()
     for q in range(CHUNKS):
         pltpu.make_async_copy(recv.at[q, pl.ds(0, SIDE - 1)], recv.at[q, pl.ds(0, SIDE - 1)], send_sem.at[q]).wait()
-        pltpu.make_async_copy(parts.at[q, pl.ds(0, MEM - 1)], parts.at[q, pl.ds(0, MEM - 1)], psend_sem.at[q]).wait()
+        span = pl.ds(q * CHUNK, CHUNK)
+        others = parts.at[pl.ds(0, MEM - 1), span]
+        pltpu.make_async_copy(others, others, psend_sem.at[q]).wait()
+        pltpu.make_async_copy(part.at[q, mine // 2, mine % 2], parts.at[mine, span], pown_sem.at[q]).wait()
+        pltpu.make_async_copy(others, others, precv_sem.at[q]).wait()
 
 
 def per_device(control, perturbation, vertical, lat_counts, lon_counts):
     bf16 = jnp.bfloat16
     dma = pltpu.SemaphoreType.DMA
-    rows = CHUNK * SHARE
-    summed = pl.pallas_call(
+    shares = pl.pallas_call(
         kernel,
-        out_shape=jax.ShapeDtypeStruct((COLS * SHARE, LAT_PAD), jnp.float32),
+        out_shape=jax.ShapeDtypeStruct((MEM, COLS, SHARE, LAT_PAD), bf16),
         in_specs=[pl.BlockSpec(memory_space=pltpu.HBM)] * 5,
-        out_specs=pl.BlockSpec(memory_space=pltpu.VMEM),
+        out_specs=pl.BlockSpec(memory_space=pltpu.HBM),
         scratch_shapes=[
             pltpu.VMEM((MEMBERS, ROWS, LEV, LON_PAD), bf16),
             pltpu.VMEM((MEMBERS, COLS, LEV, LAT_PAD), bf16),
@@ -308,15 +306,14 @@
             pltpu.VMEM((CHUNKS, SIDE - 1, SIDE, BLOCK, LANES), bf16),
             pltpu.VMEM((CHUNKS, SIDE, SIDE, BLOCK, LANES), bf16),
             pltpu.VMEM((GRID * BLOCK, LANES), jnp.float32),
-            pltpu.VMEM((CHUNKS, MEM // 2, 2, rows, LAT_PAD), bf16),
-            pltpu.VMEM((CHUNKS, MEM, rows, LAT_PAD), bf16),
+            pltpu.VMEM((CHUNKS, MEM // 2, 2, CHUNK, SHARE, LAT_PAD), bf16),
             dma((5,)), dma((len(PIECES),)), dma((len(PIECES),)), dma((CHUNKS,)), dma((CHUNKS,)), dma((CHUNKS,)),
             dma((len(PIECES),)), dma((CHUNKS,)), dma((CHUNKS,)), dma((CHUNKS,)), dma((1,)), dma((1,)), dma((1,)),
         ],
         compiler_params=pltpu.CompilerParams(collective_id=0, has_side_effects=True, vmem_limit_bytes=60 * 1024 * 1024),
     )(jnp.transpose(control, (0, 2, 1, 3)), jnp.transpose(perturbation, (0, 2, 1, 3)), vertical,
       lat_counts.reshape(1, GRID), lon_counts.reshape(1, GRID))
-    return jnp.transpose(summed.reshape(COLS, SHARE, LAT_PAD), (1, 0, 2))
+    return jnp.transpose(jnp.sum(shares.astype(jnp.float32), axis=0), (1, 0, 2))
 
 
 def solution(mesh):

time: 49.4 us -> 48.8 us (0.988)
  other arithmetic: 0 us -> 1.74 us
  local copies, waits for them, and re-layouts: 1.54 us -> 0 us
  Pallas kernels: 47.6 us -> 46.9 us
    reduce_sum x0 -> x1, other arithmetic: none -> 1.74 us  [per_device(): return jnp.transpose(jnp.sum(shares.astype(jnp.float32), axis=0), (1, 0, 2))]
    reshape x1 -> x0, local copies, waits for them, and re-layouts: 1.54 us -> none  [per_device(): return jnp.transpose(summed.reshape(COLS, SHARE, LAT_PAD), (1, 0, 2))]
    pallas_call x1, Pallas kernels: 47.6 us -> 46.9 us  [per_device(): pl.pallas_call(kernel, out_shape=jax.ShapeDtypeStruct((MEM, COLS, SHARE,...]
where the time goes in v5:
time: 48.8 us; the launch traced here: 48.7 us
  Pallas kernels  46.9 us (96%)
  other arithmetic  1.74 us (4%)
    pallas_call x1, Pallas kernels, per_device(): pl.pallas_call(kernel, out_shape=jax.ShapeDtypeStruct((MEM, COLS, SHARE,...  46.9 us
    reduce_sum x1, other arithmetic, per_device(): return jnp.transpose(jnp.sum(shares.astype(jnp.float32), axis=0), (1, 0, 2))  1.74 us

profile of v5, /device:TPU:1, one launch (start us, length us, event | category | flops | bytes accessed | tf_op | source)
XLA Modules:
  0.0 48.7 jit_solution(12280116391693225035)
XLA Ops:
  0.0 46.9 %shard_map.55 = bf16[8,12,4,384]{3,2,1,0:T(4,128)(2,1)} custom-call(bf16[4,6,32,768]{3,2,1,0:T(8,128)(2,1)} %bitcast.5, bf16[4,12,32,384]{3,2,1,0:T(8,128)(2,1)} %bitcast.6, bf16[32,32]{1,0:T(8,128)(2,1)} %vertical.1, s32[1,64]{1,0:T(1,128)} %bitcast.7, s32[1,64]{1,0:T(1,128)} %bitcast.8), custom_call_target="tpu_custom_call" | custom-call | tf_op jit(solution)/shard_map/pallas_call | solution.py:291
  46.9 1.7 %convert_reduce_fusion = f32[12,4,384]{2,1,0:T(4,128)} fusion(bf16[8,12,4,384]{3,2,1,0:T(4,128)(2,1)} %shard_map.55), kind=kLoop, calls=%fused_computation | loop fusion | flops 276480 | bytes 368640 | tf_op jit(solution)/shard_map/reduce_sum | solution.py:316

commit v6 on v5

--- a/solution.py
+++ b/solution.py
@@ -33,7 +33,7 @@
 BLOCK = CHUNK * ROWS
 SHARE = LEV // MEM
 TILE = 8
-PIECES = ((1, 0, 3), (2, 0, 3))
+PIECES = ((1, 0, 1), (1, 1, 2), (2, 0, 3))
 
 
 def nt(a, b):
@@ -208,9 +208,10 @@
     send_column()
     smooth_chunk(1)
     send_piece(0)
+    send_piece(1)
     send_direct(1)
     smooth_chunk(2)
-    send_piece(1)
+    send_piece(2)
     send_direct(2)
     for q in range(1, CHUNKS):
         keep(q)
@@ -237,8 +238,9 @@
     mixing = jnp.where(iota((LANES, LANES), 0) // LEV == iota((LANES, LANES), 1) // LEV, wide_factor, 0.0).astype(jnp.bfloat16)
 
     pass_on(0)
+    pass_on(1)
     pass_column()
-    pass_on(1)
+    pass_on(2)
 
     loads[4].wait()
     for q in range(CHUNKS):

time: 48.8 us -> 48.9 us (level)
  no operation moved by 1% of the time
where the time goes in v6:
time: 48.9 us; the launch traced here: 48.7 us
  Pallas kernels  47 us (96%)
  other arithmetic  1.74 us (4%)
    pallas_call x1, Pallas kernels, per_device(): pl.pallas_call(kernel, out_shape=jax.ShapeDtypeStruct((MEM, COLS, SHARE,...  47 us
    reduce_sum x1, other arithmetic, per_device(): return jnp.transpose(jnp.sum(shares.astype(jnp.float32), axis=0), (1, 0, 2))  1.74 us

profile of v6, /device:TPU:1, one launch (start us, length us, event | category | flops | bytes accessed | tf_op | source)
XLA Modules:
  0.0 48.7 jit_solution(16528905767859696866)
XLA Ops:
  0.0 47.0 %shard_map.55 = bf16[8,12,4,384]{3,2,1,0:T(4,128)(2,1)} custom-call(bf16[4,6,32,768]{3,2,1,0:T(8,128)(2,1)} %bitcast.5, bf16[4,12,32,384]{3,2,1,0:T(8,128)(2,1)} %bitcast.6, bf16[32,32]{1,0:T(8,128)(2,1)} %vertical.1, s32[1,64]{1,0:T(1,128)} %bitcast.7, s32[1,64]{1,0:T(1,128)} %bitcast.8), custom_call_target="tpu_custom_call" | custom-call | tf_op jit(solution)/shard_map/pallas_call | solution.py:293
  47.0 1.7 %convert_reduce_fusion = f32[12,4,384]{2,1,0:T(4,128)} fusion(bf16[8,12,4,384]{3,2,1,0:T(4,128)(2,1)} %shard_map.55), kind=kLoop, calls=%fused_computation | loop fusion | flops 276480 | bytes 368640 | tf_op jit(solution)/shard_map/reduce_sum | solution.py:318

commit v7 on v5

--- a/solution.py
+++ b/solution.py
@@ -79,7 +79,7 @@
 
 def kernel(control, perturbation, vertical, lat_counts, lon_counts, parts,
            ctrl, pert, vert, latc, lonc, lon_t, lat_k, send, column, middle, recv, wide, part,
-           in_sem, mid_send_sem, mid_recv_sem, send_sem, recv_sem, own_sem, near_sem, psend_sem, precv_sem, pown_sem, col_send_sem, col_recv_sem, col_own_sem):
+           in_sem, mid_send_sem, mid_recv_sem, send_sem, recv_sem, own_sem, near_sem, psend_sem, precv_sem, pown_sem, col_send_sem, col_recv_sem, col_own_sem, dir_send_sem, dir_recv_sem):
     me = lax.axis_index("grid")
     mine = lax.axis_index("mem")
     my_y, my_x, my_z = me // SIDE, (me % SIDE) // 2, me % 2
@@ -129,12 +129,14 @@
             for parity, block in enumerate(interleave(first, second)):
                 send[q, :, :, parity, pair * TILE:(pair + 1) * TILE, :] = block.astype(jnp.bfloat16).reshape(SIDE, 4, TILE, LANES)
 
-    def send_direct(q):
+    later = pl.ds(1, CHUNKS - 1)
+
+    def send_direct():
         def direct(step, carry):
             peer, to_y = along(step)
             pltpu.make_async_remote_copy(
-                src_ref=send.at[q, to_y, my_x, my_z], dst_ref=recv.at[q, my_y, 0],
-                send_sem=send_sem.at[q], recv_sem=recv_sem.at[q],
+                src_ref=send.at[later, to_y, my_x, my_z], dst_ref=recv.at[later, my_y, 0],
+                send_sem=dir_send_sem.at[0], recv_sem=dir_recv_sem.at[0],
                 device_id={"grid": peer}, device_id_type=MESH).start()
             return carry
 
@@ -208,10 +210,9 @@
     send_column()
     smooth_chunk(1)
     send_piece(0)
-    send_direct(1)
     smooth_chunk(2)
     send_piece(1)
-    send_direct(2)
+    send_direct()
     for q in range(1, CHUNKS):
         keep(q)
 
@@ -242,6 +243,9 @@
 
     loads[4].wait()
     for q in range(CHUNKS):
+        if q == 1:
+            straight = recv.at[later, pl.ds(0, SIDE - 1), 0]
+            pltpu.make_async_copy(straight, straight, dir_recv_sem.at[0]).wait()
         if q == 0:
             settle.wait()
         else:
@@ -250,7 +254,8 @@
             if chunk == q:
                 span = pl.ds(group * TILE, groups * TILE)
                 pltpu.make_async_copy(middle.at[q, :, my_y, span], recv.at[q, my_y, pl.ds(1, SIDE - 1), span], near_sem.at[piece]).wait()
-        pltpu.make_async_copy(recv.at[q, pl.ds(0, SIDE - 1)], recv.at[q, pl.ds(0, SIDE - 1)], recv_sem.at[q]).wait()
+        some = recv.at[q, pl.ds(0, SIDE - 1), pl.ds(0, SIDE if q == 0 else SIDE - 1)]
+        pltpu.make_async_copy(some, some, recv_sem.at[q]).wait()
         wide[...] = recv[q].astype(jnp.float32).reshape(GRID * BLOCK, LANES)
         mixed = []
         for c in range(CHUNK):
@@ -272,12 +277,15 @@
                 device_id={"mem": peer}, device_id_type=MESH).start()
         pltpu.make_async_copy(part.at[q, mine // 2, mine % 2], parts.at[mine, span], pown_sem.at[q]).start()
 
+    straight = recv.at[later, pl.ds(0, SIDE - 1), 0]
+    pltpu.make_async_copy(straight, straight, dir_send_sem.at[0]).wait()
     pltpu.make_async_copy(column.at[pl.ds(0, SIDE - 1)], column.at[pl.ds(0, SIDE - 1)], col_send_sem.at[0]).wait()
     for piece, (q, group, groups) in enumerate(PIECES):
         span = pl.ds(group * TILE, groups * TILE)
         pltpu.make_async_copy(middle.at[q, :, :, span], middle.at[q, :, :, span], mid_send_sem.at[piece]).wait()
     for q in range(CHUNKS):
-        pltpu.make_async_copy(recv.at[q, pl.ds(0, SIDE - 1)], recv.at[q, pl.ds(0, SIDE - 1)], send_sem.at[q]).wait()
+        some = recv.at[q, pl.ds(0, SIDE - 1), pl.ds(0, SIDE if q == 0 else SIDE - 1)]
+        pltpu.make_async_copy(some, some, send_sem.at[q]).wait()
         span = pl.ds(q * CHUNK, CHUNK)
         others = parts.at[pl.ds(0, MEM - 1), span]
         pltpu.make_async_copy(others, others, psend_sem.at[q]).wait()
@@ -308,7 +316,7 @@
             pltpu.VMEM((GRID * BLOCK, LANES), jnp.float32),
             pltpu.VMEM((CHUNKS, MEM // 2, 2, CHUNK, SHARE, LAT_PAD), bf16),
             dma((5,)), dma((len(PIECES),)), dma((len(PIECES),)), dma((CHUNKS,)), dma((CHUNKS,)), dma((CHUNKS,)),
-            dma((len(PIECES),)), dma((CHUNKS,)), dma((CHUNKS,)), dma((CHUNKS,)), dma((1,)), dma((1,)), dma((1,)),
+            dma((len(PIECES),)), dma((CHUNKS,)), dma((CHUNKS,)), dma((CHUNKS,)), dma((1,)), dma((1,)), dma((1,)), dma((1,)), dma((1,)),
         ],
         compiler_params=pltpu.CompilerParams(collective_id=0, has_side_effects=True, vmem_limit_bytes=60 * 1024 * 1024),
     )(jnp.transpose(control, (0, 2, 1, 3)), jnp.transpose(perturbation, (0, 2, 1, 3)), vertical,

time: 48.8 us -> 48.9 us (level)
  no operation moved by 1% of the time
where the time goes in v7:
time: 48.9 us; the launch traced here: 48.7 us
  Pallas kernels  47 us (96%)
  other arithmetic  1.74 us (4%)
    pallas_call x1, Pallas kernels, per_device(): pl.pallas_call(kernel, out_shape=jax.ShapeDtypeStruct((MEM, COLS, SHARE,...  47 us
    reduce_sum x1, other arithmetic, per_device(): return jnp.transpose(jnp.sum(shares.astype(jnp.float32), axis=0), (1, 0, 2))  1.74 us

profile of v7, /device:TPU:1, one launch (start us, length us, event | category | flops | bytes accessed | tf_op | source)
XLA Modules:
  0.0 48.7 jit_solution(6356727156879874283)
XLA Ops:
  0.0 47.0 %shard_map.55 = bf16[8,12,4,384]{3,2,1,0:T(4,128)(2,1)} custom-call(bf16[4,6,32,768]{3,2,1,0:T(8,128)(2,1)} %bitcast.5, bf16[4,12,32,384]{3,2,1,0:T(8,128)(2,1)} %bitcast.6, bf16[32,32]{1,0:T(8,128)(2,1)} %vertical.1, s32[1,64]{1,0:T(1,128)} %bitcast.7, s32[1,64]{1,0:T(1,128)} %bitcast.8), custom_call_target="tpu_custom_call" | custom-call | tf_op jit(solution)/shard_map/pallas_call | solution.py:299
  47.0 1.7 %convert_reduce_fusion = f32[12,4,384]{2,1,0:T(4,128)} fusion(bf16[8,12,4,384]{3,2,1,0:T(4,128)(2,1)} %shard_map.55), kind=kLoop, calls=%fused_computation | loop fusion | flops 276480 | bytes 368640 | tf_op jit(solution)/shard_map/reduce_sum | solution.py:324
